TPU v7x, 32 devices: a whole 2x2x4 slice. The times are simulated.
32 devices in a mesh: outer: 4 (over y, x), inner: 8 (over z, core).
Axes of the slice: x: 2, y: 2, z: 4, core: 2. Of those that a mesh axis runs over, the one named last changes fastest.
Arguments:
- p_factor: bfloat16 [56, 56, 16384], P('outer', None, 'inner'), may hold values from -24 to 24
- q_factor: bfloat16 [56, 56, 16384], P(None, None, 'inner'), may hold values from -6 to 6
- truncation: bfloat16 [3136, 56], P('outer'), may hold values from -0.109375 to 0.109375
Outputs:
- gram: float32 [3136, 3136], P('outer', 'inner')
- coarse: float32 [56, 16384], P(None, 'inner')
All inputs are finite; a program needn't handle non-finite values.
Results may differ from a plain program's by a relative error of at most 0.003.
Values may be sent and summed in bfloat16 or wider, within the bound.
No kernel may reach another device: no remote copies, remote signals or barrier semaphores. Data moves between devices by JAX's collectives and lax.ppermute only.
A program may use at most 128 MiB of HBM per device.

v0:
```python
import math
import jax
import jax.numpy as jnp
from jax import lax
from jax.sharding import PartitionSpec as P


def contract(factor, q_factor):
    bond_size = q_factor.shape[0]
    paired = jnp.einsum("imc,jmc->ijc", factor, q_factor, preferred_element_type=jnp.float32)
    paired = paired / math.sqrt(q_factor.shape[1])
    return paired.reshape(factor.shape[0] * bond_size, factor.shape[2]).astype(jnp.bfloat16)


def body(p_factor, q_factor, truncation):
    columns = p_factor.shape[2]
    own_rows = contract(p_factor, q_factor)
    gathered = lax.all_gather(own_rows, "outer", axis=0, tiled=True)
    partial_value = lax.dot_general(
        own_rows, gathered, (((1,), (1,)), ((), ())), preferred_element_type=jnp.float32
    )
    total_columns = columns * lax.axis_size("inner")
    gram = lax.psum_scatter(partial_value, "inner", scatter_dimension=1, tiled=True) / total_columns
    local_term = lax.dot_general(
        truncation, own_rows, (((0,), (0,)), ((), ())), preferred_element_type=jnp.float32
    )
    absorbed = lax.psum(local_term, "outer")
    squares = lax.psum(jnp.sum(absorbed * absorbed), "inner")
    norm_scale = jnp.sqrt(squares / (absorbed.shape[0] * total_columns) + 1e-06)
    return (gram, absorbed / norm_scale)


def solution(mesh):
    return jax.shard_map(
        body,
        mesh=mesh,
        in_specs=(P("outer", None, "inner"), P(None, None, "inner"), P("outer", None)),
        out_specs=(P("outer", "inner"), P(None, "inner")),
        check_vma=False,
    )
```

profile of v0, /device:TPU:0, one launch (start us, length us, event | category | flops | bytes accessed | tf_op | source)
XLA Modules:
  0.0 385.2 jit_solution(4690721399324301520)
XLA Ops:
  7.2 0.0 copy-start
  7.2 0.0 all-gather.2.cloned.1.call-start
  7.2 10.5 %copy.11 = bf16[14,56,2048]{1,0,2:T(8,128)(2,1)} copy(bf16[14,56,2048]{2,1,0:T(8,128)(2,1)} %param.3) | data formatting | bytes 6422528 | tf_op args[0]
  17.7 31.2 %copy.10 = bf16[56,56,2048]{1,0,2:T(8,128)(2,1)} copy(bf16[56,56,2048]{2,1,0:T(8,128)(2,1)} %param.4) | data formatting | bytes 25690112 | tf_op args[1]
  48.9 22.2 %fusion = bf16[14,56,2048]{1,0,2:T(8,128)(2,1)} fusion(bf16[56,56,2048]{1,0,2:T(8,128)(2,1)} %copy.10, bf16[14,56,2048]{1,0,2:T(8,128)(2,1)} %copy.11), kind=kOutput, calls=%fused_computation.1 | convolution fusion | flops 183042048 | bytes 19267584 | tf_op jit(solution)/shard_map/imc,jmc->ijc/dot_general | solution.py:10
  71.1 9.8 %copy.12 = bf16[14,56,2048]{2,1,0:T(8,128)(2,1)} copy(bf16[14,56,2048]{1,0,2:T(8,128)(2,1)} %fusion) | data formatting | bytes 6422528 | tf_op jit(solution)/shard_map/convert_element_type | solution.py:12
  80.9 0.0 copy-start.2
  80.9 0.0 all-gather.2.cloned.1.call-update
  80.9 0.0 all-reduce.3.cloned.1.call-start
  81.0 0.0 copy-done
  81.0 3.6 convolution_bitcast_fusion
  84.6 0.0 all-reduce.3.cloned.1.call-update
  84.6 0.0 reduce-scatter.4.cloned.1.call-start
  84.6 123.9 %all-gather.2.cloned.1.call-done = bf16[3136,2048]{1,0:T(8,128)(2,1)} async-done(((bf16[784,2048]{1,0:T(8,128)(2,1)}), bf16[3136,2048]{1,0:T(8,128)(2,1)}) %all-gather.2.cloned.1.call-update) | async-done | bytes 12845072 | tf_op jit(solution)/shard_map/all_gather | solution.py:18
  208.5 0.0 copy-done.2
  208.5 0.0 copy-start.1
  208.5 18.2 %fusion.1 = f32[784,3136]{0,1:T(8,128)} fusion(bf16[784,2048]{1,0:T(8,128)(2,1)S(1)} %bitcast.14, bf16[3136,2048]{1,0:T(8,128)(2,1)} %all-gather.2.cloned.1.call-done), kind=kOutput, calls=%fused_computation.6 | convolution fusion | flops 10070523904 | bytes 25890816 | tf_op jit(solution)/shard_map/dot_general | solution.py:19
  226.7 0.0 reduce-scatter.4.cloned.1.call-update
  226.8 30.0 %all-reduce.3.cloned.1.call-done = f32[56,2048]{1,0:T(8,128)} async-done(((f32[56,2048]{1,0:T(8,128)}), f32[56,2048]{1,0:T(8,128)}) %all-reduce.3.cloned.1.call-update) | async-done | bytes 458768 | tf_op jit(solution)/shard_map/psum | solution.py:27
  256.8 1.7 multiply_reduce_fusion
  258.5 16.8 %psum.15 = f32[]{:T(128)} all-reduce(f32[]{:T(128)} %multiply_reduce_fusion), channel_id=1, replica_groups=mesh['outer'=4,'inner'=8] {'inner'}, use_global_device_ids=true, to_apply=%region_3.0 | all-reduce | flops 1 | bytes 8 | tf_op jit(solution)/shard_map/psum | solution.py:28
  276.0 1.8 broadcast_divide_fusion
  277.8 98.4 %reduce-scatter.4.cloned.1.call-done = f32[784,392]{0,1:T(8,128)} async-done(((f32[784,3136]{0,1:T(8,128)}), f32[784,392]{0,1:T(8,128)}) %reduce-scatter.4.cloned.1.call-update) | async-done | bytes 1229328
  376.2 2.5 broadcast_multiply_fusion
  378.7 0.0 copy-done.1
Async XLA Ops:
  7.2 73.8 %copy-start = (bf16[784,56]{0,1:T(8,128)(2,1)S(1)}, bf16[784,56]{0,1:T(8,128)(2,1)}, u32[]{:S(2)}) copy-start(bf16[784,56]{0,1:T(8,128)(2,1)} %param.5) | copy-start | bytes 263428
  7.2 201.3 %all-gather.2.cloned.1.call-start = ((), (), s32[]{:S(2)}) async-start(), calls=%async_computation.1 | async-start | bytes 16056320 | tf_op jit(solution)/shard_map/all_gather | solution.py:18
  80.9 127.6 %copy-start.2 = (bf16[14,56,2048]{2,1,0:T(8,128)(2,1)S(1)}, bf16[14,56,2048]{2,1,0:T(8,128)(2,1)}, u32[]{:S(2)}) copy-start(bf16[14,56,2048]{2,1,0:T(8,128)(2,1)} %copy.12) | copy-start | bytes 9633796
  80.9 175.8 %all-reduce.3.cloned.1.call-start = ((), (), s32[]{:S(2)}) async-start(), calls=%async_computation.2 | async-start | bytes 917504 | tf_op jit(solution)/shard_map/psum | solution.py:27
  84.6 291.6 %reduce-scatter.4.cloned.1.call-start = ((), (), s32[]{:S(2)}) async-start(), calls=%async_computation.3 | async-start | bytes 12644352
  208.5 170.2 %copy-start.1 = (bf16[784,56]{0,1:T(8,128)(2,1)S(1)}, bf16[784,56]{0,1:T(8,128)(2,1)}, u32[]{:S(2)}) copy-start(bf16[784,56]{0,1:T(8,128)(2,1)} %param.5) | copy-start | bytes 263428
Sparse Core Ops, SparseCore 0:
  81.1 127.3 all-gather.1
  212.1 44.6 all-reduce.2
  259.2 116.9 reduce-scatter.3
where the time goes:
time: 387 us; the launch traced here: 385 us
  waiting for transfers between devices  252 us (65%)
  local copies, waits for them, and re-layouts  51.5 us (13%)
  matrix products  44 us (11%)
  blocking collectives  16.8 us (4%)
  between operations  14.5 us (4%)
  other arithmetic  6.09 us (2%)
    all_gather x1, waiting for transfers between devices, body(): gathered = lax.all_gather(own_rows, 'outer', axis=0, tiled=True)  124 us
    unnamed x4, waiting for transfers between devices  98.4 us
    unnamed x8, local copies, waits for them, and re-layouts  41.7 us
    psum x1, waiting for transfers between devices, body(): absorbed = lax.psum(local_term, 'outer')  30 us
    dot_general x1, matrix products, contract(): jnp.einsum('imc,jmc->ijc', factor, q_factor, preferred_element_type=jnp.f...  22.2 us
    dot_general x1, matrix products, body(): lax.dot_general(own_rows, gathered, (((1,), (1,)), ((), ())), preferred_e...  18.2 us
    psum x1, blocking collectives, body(): squares = lax.psum(jnp.sum(absorbed * absorbed), 'inner')  16.8 us
    convert_element_type x1, local copies, waits for them, and re-layouts, contract(): paired.reshape(factor.shape[0] * bond_size, factor.shape[2])  9.78 us
  transfers between devices with their start and end apart: 3, of which 3 were waited for; matrix products, arithmetic and copies ran while one was open for 7% of the time, Pallas kernels for 0%

commit v1 on v0

--- a/solution.py
+++ b/solution.py
@@ -24,7 +24,7 @@
     local_term = lax.dot_general(
         truncation, own_rows, (((0,), (0,)), ((), ())), preferred_element_type=jnp.float32
     )
-    absorbed = lax.psum(local_term, "outer")
+    absorbed = jnp.sum(lax.all_gather(local_term, "outer"), axis=0)
     squares = lax.psum(jnp.sum(absorbed * absorbed), "inner")
     norm_scale = jnp.sqrt(squares / (absorbed.shape[0] * total_columns) + 1e-06)
     return (gram, absorbed / norm_scale)

time: 387 us -> 374 us (0.966)
  waiting for transfers between devices: 252 us -> 239 us
    psum x1 -> x0, waiting for transfers between devices: 30 us -> none  [body(): absorbed = lax.psum(local_term, 'outer')]
    all_gather x0 -> x1, waiting for transfers between devices: none -> 17.3 us  [body(): absorbed = jnp.sum(lax.all_gather(local_term, 'outer'), axis=0)]
where the time goes in v1:
time: 374 us; the launch traced here: 372 us
  waiting for transfers between devices  239 us (64%)
  local copies, waits for them, and re-layouts  51.5 us (14%)
  matrix products  44 us (12%)
  blocking collectives  17.2 us (5%)
  between operations  14.5 us (4%)
  other arithmetic  5.71 us (2%)
    all_gather x1, waiting for transfers between devices, body(): gathered = lax.all_gather(own_rows, 'outer', axis=0, tiled=True)  124 us
    unnamed x4, waiting for transfers between devices  98.3 us
    unnamed x8, local copies, waits for them, and re-layouts  41.7 us
    dot_general x1, matrix products, contract(): jnp.einsum('imc,jmc->ijc', factor, q_factor, preferred_element_type=jnp.f...  22.2 us
    dot_general x1, matrix products, body(): lax.dot_general(own_rows, gathered, (((1,), (1,)), ((), ())), preferred_e...  18.2 us
    all_gather x1, waiting for transfers between devices, body(): absorbed = jnp.sum(lax.all_gather(local_term, 'outer'), axis=0)  17.3 us
    psum x1, blocking collectives, body(): squares = lax.psum(jnp.sum(absorbed * absorbed), 'inner')  17.2 us
    convert_element_type x1, local copies, waits for them, and re-layouts, contract(): paired.reshape(factor.shape[0] * bond_size, factor.shape[2])  9.78 us
  transfers between devices with their start and end apart: 3, of which 3 were waited for; matrix products, arithmetic and copies ran while one was open for 7% of the time, Pallas kernels for 0%

profile of v1, /device:TPU:0, one launch (start us, length us, event | category | flops | bytes accessed | tf_op | source)
XLA Modules:
  0.0 372.5 jit_solution(10731519565874705026)
XLA Ops:
  7.2 0.0 copy-start
  7.2 0.0 all-gather.4.cloned.1.call-start
  7.2 10.5 %copy.11 = bf16[14,56,2048]{1,0,2:T(8,128)(2,1)} copy(bf16[14,56,2048]{2,1,0:T(8,128)(2,1)} %param.3) | data formatting | bytes 6422528 | tf_op args[0]
  17.7 31.2 %copy.10 = bf16[56,56,2048]{1,0,2:T(8,128)(2,1)} copy(bf16[56,56,2048]{2,1,0:T(8,128)(2,1)} %param.4) | data formatting | bytes 25690112 | tf_op args[1]
  48.9 22.2 %fusion = bf16[14,56,2048]{1,0,2:T(8,128)(2,1)} fusion(bf16[56,56,2048]{1,0,2:T(8,128)(2,1)} %copy.10, bf16[14,56,2048]{1,0,2:T(8,128)(2,1)} %copy.11), kind=kOutput, calls=%fused_computation.1 | convolution fusion | flops 183042048 | bytes 19267584 | tf_op jit(solution)/shard_map/imc,jmc->ijc/dot_general | solution.py:10
  71.1 9.8 %copy.12 = bf16[14,56,2048]{2,1,0:T(8,128)(2,1)} copy(bf16[14,56,2048]{1,0,2:T(8,128)(2,1)} %fusion) | data formatting | bytes 6422528 | tf_op jit(solution)/shard_map/convert_element_type | solution.py:12
  80.9 0.0 copy-start.2
  80.9 0.0 all-gather.4.cloned.1.call-update
  80.9 0.0 all-gather.6.cloned.1.call-start
  81.0 0.0 copy-done
  81.0 3.6 convolution_bitcast_fusion
  84.6 0.0 all-gather.6.cloned.1.call-update
  84.6 0.0 reduce-scatter.4.cloned.1.call-start
  84.6 123.8 %all-gather.4.cloned.1.call-done = bf16[3136,2048]{1,0:T(8,128)(2,1)} async-done(((bf16[784,2048]{1,0:T(8,128)(2,1)}), bf16[3136,2048]{1,0:T(8,128)(2,1)}) %all-gather.4.cloned.1.call-update) | async-done | bytes 12845072 | tf_op jit(solution)/shard_map/all_gather | solution.py:18
  208.5 0.0 copy-done.2
  208.5 18.2 %fusion.1 = f32[784,3136]{0,1:T(8,128)} fusion(bf16[784,2048]{1,0:T(8,128)(2,1)S(1)} %bitcast.15, bf16[3136,2048]{1,0:T(8,128)(2,1)} %all-gather.4.cloned.1.call-done), kind=kOutput, calls=%fused_computation.6 | convolution fusion | flops 10070523904 | bytes 25890816 | tf_op jit(solution)/shard_map/dot_general | solution.py:19
  226.7 0.0 copy-start.1
  226.7 0.0 reduce-scatter.4.cloned.1.call-update
  226.7 17.3 %all-gather.6.cloned.1.call-done = f32[224,2048]{1,0:T(8,128)} async-done(((f32[56,2048]{1,0:T(8,128)}), f32[224,2048]{1,0:T(8,128)}) %all-gather.6.cloned.1.call-update) | async-done | bytes 1835024 | tf_op jit(solution)/shard_map/all_gather | solution.py:27
  244.1 1.7 reduce_sum.18
  245.8 0.7 multiply_reduce_fusion
  246.5 17.2 %psum.7 = f32[]{:T(128)} all-reduce(f32[]{:T(128)} %multiply_reduce_fusion), channel_id=1, replica_groups=mesh['outer'=4,'inner'=8] {'inner'}, use_global_device_ids=true, to_apply=%region_3.0 | all-reduce | flops 1 | bytes 8 | tf_op jit(solution)/shard_map/psum | solution.py:28
  264.3 0.8 broadcast_divide_fusion
  265.2 98.3 %reduce-scatter.4.cloned.1.call-done = f32[784,392]{0,1:T(8,128)} async-done(((f32[784,3136]{0,1:T(8,128)}), f32[784,392]{0,1:T(8,128)}) %reduce-scatter.4.cloned.1.call-update) | async-done | bytes 1229328
  363.4 2.5 broadcast_multiply_fusion
  365.9 0.0 copy-done.1
Async XLA Ops:
  7.2 73.8 %copy-start = (bf16[784,56]{0,1:T(8,128)(2,1)S(1)}, bf16[784,56]{0,1:T(8,128)(2,1)}, u32[]{:S(2)}) copy-start(bf16[784,56]{0,1:T(8,128)(2,1)} %param.5) | copy-start | bytes 263428
  7.2 201.3 %all-gather.4.cloned.1.call-start = ((), (), s32[]{:S(2)}) async-start(), calls=%async_computation.1 | async-start | bytes 16056320 | tf_op jit(solution)/shard_map/all_gather | solution.py:18
  80.9 127.6 %copy-start.2 = (bf16[14,56,2048]{2,1,0:T(8,128)(2,1)S(1)}, bf16[14,56,2048]{2,1,0:T(8,128)(2,1)}, u32[]{:S(2)}) copy-start(bf16[14,56,2048]{2,1,0:T(8,128)(2,1)} %copy.12) | copy-start | bytes 9633796
  80.9 163.1 %all-gather.6.cloned.1.call-start = ((), (), s32[]{:S(2)}) async-start(), calls=%async_computation.2 | async-start | bytes 2293760 | tf_op jit(solution)/shard_map/all_gather | solution.py:27
  84.6 278.8 %reduce-scatter.4.cloned.1.call-start = ((), (), s32[]{:S(2)}) async-start(), calls=%async_computation.3 | async-start | bytes 12644352
  226.7 139.2 %copy-start.1 = (bf16[784,56]{0,1:T(8,128)(2,1)S(1)}, bf16[784,56]{0,1:T(8,128)(2,1)}, u32[]{:S(2)}) copy-start(bf16[784,56]{0,1:T(8,128)(2,1)} %param.5) | copy-start | bytes 263428
Sparse Core Ops, SparseCore 0:
  81.1 127.3 all-gather.3
  210.9 33.1 all-gather.5
  246.4 116.9 reduce-scatter.3
